TPU v7x, 128 devices: a whole 4x4x4 slice. The times are simulated.
128 devices in a mesh: expert: 8 (over z_lo, x), shard: 16 (over z_hi, y, core).
Axes of the slice: x: 4, y: 4, z: 4 (z_hi: 2, z_lo: 2; z = z_hi * 2 + z_lo), core: 2. Of those that a mesh axis runs over, the one named last changes fastest.
Arguments:
- grad_out: bfloat16 [8, 2048, 3072], P('expert', 'shard'), may hold values from -6 to 6
- gate_pre: bfloat16 [8, 2048, 8192], P('expert', None, 'shard'), may hold values from -8 to 8
- up_pre: bfloat16 [8, 2048, 8192], P('expert', None, 'shard'), may hold values from -6 to 6
- counts: int32 [8, 16], P('expert', 'shard'), may hold values from 32 to 128
- placement: int32 [8], replicated, may hold values from 0 to 63, as said below
- master: float32 [8, 8192, 3072], P('expert', 'shard')
Outputs:
- d_gate: bfloat16 [8, 2048, 8192], P('expert', None, 'shard')
- d_up: bfloat16 [8, 2048, 8192], P('expert', None, 'shard')
- new_master: float32 [8, 8192, 3072], P('expert', 'shard')
Inputs may be any that keep to these rules, and one draw needn't show every extreme that they name: `placement`: slots that hold the same expert form aligned blocks of 1, 2 or 4 consecutive slots, each block starting at a multiple of its size; different blocks hold different experts.
All inputs are finite; a program needn't handle non-finite values.
Results may differ from a plain program's by a relative error of at most 0.006.
Values may be sent and summed in bfloat16 or wider, within the bound.
A program may use at most 256 MiB of HBM per device.

v0:
```python
import jax
import jax.numpy as jnp
from jax import lax
from jax.sharding import PartitionSpec as P

learn_rate = 0.02
rms_eps = 1e-06
pieces = 6


def from_partner(shard, axis, flip):
    return lax.ppermute(shard, axis, [(i, i ^ flip) for i in range(lax.axis_size(axis))])


def per_device(grad_out, gate_pre, up_pre, counts, placement, master):
    weight_work = master[0].astype(jnp.bfloat16)
    local_rows, width = (grad_out.shape[1], grad_out.shape[2])
    row_valid = (jnp.arange(local_rows, dtype=jnp.int32) < counts[0, 0]).astype(jnp.bfloat16)
    masked = grad_out[0] * row_valid[:, None]
    gate_val = gate_pre[0].astype(jnp.float32)
    up_val = up_pre[0].astype(jnp.float32)
    gate_sig = jax.nn.sigmoid(gate_val)
    gate_act = gate_val * gate_sig
    gate_slope = gate_sig * (1.0 + gate_val * (1.0 - gate_sig))
    hidden = (gate_act * up_val).astype(jnp.bfloat16)
    my_slot = lax.axis_index("expert")
    slot_order = jnp.arange(placement.shape[0], dtype=jnp.int32)

    def expert_of(slot):
        return jnp.sum(jnp.where(slot_order == slot, placement, 0))

    my_expert = expert_of(my_slot)
    same_pair = my_expert == expert_of(my_slot ^ 1)
    same_quad = my_expert == expert_of(my_slot ^ 3)
    step = width // pieces
    d_hidden = 0.0
    sums = []
    for piece in range(pieces):
        cols = slice(piece * step, (piece + 1) * step)
        rows = lax.all_gather(masked[:, cols], "shard", axis=0, tiled=True)
        grad = lax.dot_general(
            hidden, rows, (((0,), (0,)), ((), ())), preferred_element_type=jnp.float32
        )
        for flip, same in ((1, same_pair), (3, same_quad)):
            received = from_partner(grad.astype(jnp.bfloat16), "expert", flip)
            grad = grad + jnp.where(same, received.astype(jnp.float32), 0.0)
        sums.append(grad)
        d_hidden = d_hidden + lax.dot_general(
            rows, weight_work[:, cols], (((1,), (1,)), ((), ())), preferred_element_type=jnp.float32
        )
    up_acc = (d_hidden * gate_act).astype(jnp.bfloat16)
    gate_acc = (d_hidden * up_val * gate_slope).astype(jnp.bfloat16)
    grad_sum = jnp.concatenate(sums, axis=1)
    row_rms = jnp.sqrt(jnp.mean(grad_sum * grad_sum, axis=1, keepdims=True) + rms_eps)
    new_master = master[0] - learn_rate * grad_sum / row_rms
    return (gate_acc[None], up_acc[None], new_master[None])


def solution(mesh):
    return jax.shard_map(
        per_device,
        mesh=mesh,
        in_specs=(
            P("expert", "shard", None),
            P("expert", None, "shard"),
            P("expert", None, "shard"),
            P("expert", "shard"),
            P(),
            P("expert", "shard", None),
        ),
        out_specs=(
            P("expert", None, "shard"),
            P("expert", None, "shard"),
            P("expert", "shard", None),
        ),
        check_vma=False,
    )
```

profile of v0, /device:TPU:0, one launch (start us, length us, event | category | flops | bytes accessed | tf_op | source)
XLA Modules:
  0.0 441.0 jit_solution(3005373433382526787)
XLA Ops:
  17.2 6.6 %copy.9 = f32[1,512,3072]{1,2,0:T(8,128)} copy(f32[1,512,3072]{2,1,0:T(8,128)} %param.11) | data formatting | bytes 12582912 | tf_op args[5]
  23.8 3.3 convert_bitcast_fusion
  27.0 35.0 %all-gather.15.cloned.1.call-done = bf16[2048,512]{1,0:T(8,128)(2,1)} async-done(((bf16[128,512]{1,0:T(8,128)(2,1)}), bf16[2048,512]{1,0:T(8,128)(2,1)}) %all-gather.15.cloned.1.call-update) | async-done | bytes 2097168 | tf_op jit(solution)/shard_map/all_gather | solution.py:40
  62.0 4.9 %fusion.17 = f32[2048,512]{1,0:T(8,128)} fusion(bf16[2048,512]{1,0:T(8,128)(2,1)} %all-gather.15.cloned.1.call-done, bf16[512,3072]{1,0:T(8,128)(2,1)S(1)} %convert_bitcast_fusion), kind=kOutput, calls=%fused_computation.46 | convolution fusion | flops 1073741824 | bytes 6815744 | tf_op jit(solution)/shard_map/dot_general | solution.py:48
  66.8 44.7 %all-gather.13.cloned.1.call-done = bf16[2048,512]{1,0:T(8,128)(2,1)} async-done(((bf16[128,512]{1,0:T(8,128)(2,1)}), bf16[2048,512]{1,0:T(8,128)(2,1)}) %all-gather.13.cloned.1.call-update) | async-done | bytes 2097168 | tf_op jit(solution)/shard_map/all_gather | solution.py:40
  111.6 4.9 %fusion.19 = f32[2048,512]{1,0:T(8,128)} fusion(bf16[2048,512]{1,0:T(8,128)(2,1)} %all-gather.13.cloned.1.call-done, bf16[512,3072]{1,0:T(8,128)(2,1)S(1)} %convert_bitcast_fusion), kind=kOutput, calls=%fused_computation.48 | convolution fusion | flops 1073741824 | bytes 6815744 | tf_op jit(solution)/shard_map/dot_general | solution.py:48
  116.5 44.7 %all-gather.11.cloned.1.call-done = bf16[2048,512]{1,0:T(8,128)(2,1)} async-done(((bf16[128,512]{1,0:T(8,128)(2,1)}), bf16[2048,512]{1,0:T(8,128)(2,1)}) %all-gather.11.cloned.1.call-update) | async-done | bytes 2097168 | tf_op jit(solution)/shard_map/all_gather | solution.py:40
  161.2 4.9 %fusion.21 = f32[2048,512]{1,0:T(8,128)} fusion(bf16[2048,512]{1,0:T(8,128)(2,1)} %all-gather.11.cloned.1.call-done, bf16[512,3072]{1,0:T(8,128)(2,1)S(1)} %convert_bitcast_fusion), kind=kOutput, calls=%fused_computation.50 | convolution fusion | flops 1073741824 | bytes 6815744 | tf_op jit(solution)/shard_map/dot_general | solution.py:48
  166.0 44.6 %all-gather.9.cloned.1.call-done = bf16[2048,512]{1,0:T(8,128)(2,1)} async-done(((bf16[128,512]{1,0:T(8,128)(2,1)}), bf16[2048,512]{1,0:T(8,128)(2,1)}) %all-gather.9.cloned.1.call-update) | async-done | bytes 2097168 | tf_op jit(solution)/shard_map/all_gather | solution.py:40
  210.6 4.8 %fusion.23 = f32[2048,512]{1,0:T(8,128)} fusion(bf16[2048,512]{1,0:T(8,128)(2,1)} %all-gather.9.cloned.1.call-done, bf16[512,3072]{1,0:T(8,128)(2,1)S(1)} %convert_bitcast_fusion), kind=kOutput, calls=%fused_computation.52 | convolution fusion | flops 1073741824 | bytes 6815744 | tf_op jit(solution)/shard_map/dot_general | solution.py:48
  215.4 44.6 %all-gather.7.cloned.1.call-done = bf16[2048,512]{1,0:T(8,128)(2,1)} async-done(((bf16[128,512]{1,0:T(8,128)(2,1)}), bf16[2048,512]{1,0:T(8,128)(2,1)}) %all-gather.7.cloned.1.call-update) | async-done | bytes 2097168 | tf_op jit(solution)/shard_map/all_gather | solution.py:40
  260.0 4.9 %fusion.25 = f32[2048,512]{1,0:T(8,128)} fusion(bf16[2048,512]{1,0:T(8,128)(2,1)} %all-gather.7.cloned.1.call-done, bf16[512,3072]{1,0:T(8,128)(2,1)S(1)} %convert_bitcast_fusion), kind=kOutput, calls=%fused_computation.54 | convolution fusion | flops 1073741824 | bytes 6815744 | tf_op jit(solution)/shard_map/dot_general | solution.py:48
  264.9 45.2 %all-gather.17.cloned.1.call-done = bf16[2048,512]{1,0:T(8,128)(2,1)} async-done(((bf16[128,512]{1,0:T(8,128)(2,1)}), bf16[2048,512]{1,0:T(8,128)(2,1)}) %all-gather.17.cloned.1.call-update) | async-done | bytes 2097168 | tf_op jit(solution)/shard_map/all_gather | solution.py:40
  310.0 12.0 %fusion.8 = (bf16[1,2048,512]{2,1,0:T(8,128)(2,1)}, bf16[1,2048,512]{2,1,0:T(8,128)(2,1)}, bf16[2048,512]{1,0:T(8,128)(2,1)S(1)}) fusion(bf16[1,2048,512]{2,1,0:T(8,128)(2,1)} %param.7, bf16[1,2048,512]{2,1,0:T(8,128)(2,1)} %param.8, bf16[2048,512]{1,0:T(8,128)(2,1)} %all-gather.17.cloned.1.call-done, bf16[512,3072]{1,0:T(8,128)(2,1)S(1)} %convert_bitcast_fusion, ...), kind=kOutput, calls=%fused_computation.18 | convolution fusion | flops 1096810496 | bytes 34078720 | tf_op jit(solution)/shard_map/dot_general | solution.py:48
  339.8 9.6 %collective-permute-done.2 = bf16[512,512]{0,1:T(8,128)(2,1)S(1)} collective-permute-done((bf16[512,512]{0,1:T(8,128)(2,1)S(1)}, bf16[512,512]{0,1:T(8,128)(2,1)S(1)}, u32[]{:S(2)}, u32[]{:S(2)}) %collective-permute-start.2) | collective-permute-done | bytes 524320 | tf_op jit(solution)/shard_map/ppermute | solution.py:12
  352.3 8.4 %collective-permute-done.4 = bf16[512,512]{0,1:T(8,128)(2,1)S(1)} collective-permute-done((bf16[512,512]{0,1:T(8,128)(2,1)S(1)}, bf16[512,512]{0,1:T(8,128)(2,1)S(1)}, u32[]{:S(2)}, u32[]{:S(2)}) %collective-permute-start.4) | collective-permute-done | bytes 524320 | tf_op jit(solution)/shard_map/ppermute | solution.py:12
  363.5 8.4 %collective-permute-done.6 = bf16[512,512]{0,1:T(8,128)(2,1)S(1)} collective-permute-done((bf16[512,512]{0,1:T(8,128)(2,1)S(1)}, bf16[512,512]{0,1:T(8,128)(2,1)S(1)}, u32[]{:S(2)}, u32[]{:S(2)}) %collective-permute-start.6) | collective-permute-done | bytes 524320 | tf_op jit(solution)/shard_map/ppermute | solution.py:12
  374.8 8.4 %collective-permute-done.8 = bf16[512,512]{0,1:T(8,128)(2,1)S(1)} collective-permute-done((bf16[512,512]{0,1:T(8,128)(2,1)S(1)}, bf16[512,512]{0,1:T(8,128)(2,1)S(1)}, u32[]{:S(2)}, u32[]{:S(2)}) %collective-permute-start.8) | collective-permute-done | bytes 524320 | tf_op jit(solution)/shard_map/ppermute | solution.py:12
  386.0 7.7 %collective-permute-done.10 = bf16[512,512]{0,1:T(8,128)(2,1)S(1)} collective-permute-done((bf16[512,512]{0,1:T(8,128)(2,1)S(1)}, bf16[512,512]{0,1:T(8,128)(2,1)S(1)}, u32[]{:S(2)}, u32[]{:S(2)}) %collective-permute-start.10) | collective-permute-done | bytes 524320 | tf_op jit(solution)/shard_map/ppermute | solution.py:12
  393.7 2.7 collective-permute-start.9
  398.4 11.4 %collective-permute-done.9 = bf16[512,512]{0,1:T(8,128)(2,1)S(1)} collective-permute-done((bf16[512,512]{0,1:T(8,128)(2,1)S(1)}, bf16[512,512]{0,1:T(8,128)(2,1)S(1)}, u32[]{:S(2)}, u32[]{:S(2)}) %collective-permute-start.9) | collective-permute-done | bytes 524320 | tf_op jit(solution)/shard_map/ppermute | solution.py:12
  410.0 9.4 %collective-permute-done.11 = bf16[512,512]{0,1:T(8,128)(2,1)S(1)} collective-permute-done((bf16[512,512]{0,1:T(8,128)(2,1)S(1)}, bf16[512,512]{0,1:T(8,128)(2,1)S(1)}, u32[]{:S(2)}, u32[]{:S(2)}) %collective-permute-start.11) | collective-permute-done | bytes 524320 | tf_op jit(solution)/shard_map/ppermute | solution.py:12
  423.4 4.2 divide_subtract_fusion
  427.6 6.6 %copy.10 = f32[1,512,3072]{2,1,0:T(8,128)} copy(f32[1,512,3072]{1,2,0:T(8,128)} %divide_subtract_fusion) | data formatting | bytes 12582912
  (75 shorter events, 41.9 us)
Async XLA Ops:
  7.2 54.8 %all-gather.15.cloned.1.call-start = ((), (), s32[]{:S(2)}) async-start(), calls=%async_computation.4 | async-start | bytes 2228224 | tf_op jit(solution)/shard_map/all_gather | solution.py:40
  10.0 101.5 %all-gather.13.cloned.1.call-start = ((), (), s32[]{:S(2)}) async-start(), calls=%async_computation.3 | async-start | bytes 2228224 | tf_op jit(solution)/shard_map/all_gather | solution.py:40
  10.8 150.4 %all-gather.11.cloned.1.call-start = ((), (), s32[]{:S(2)}) async-start(), calls=%async_computation.2 | async-start | bytes 2228224 | tf_op jit(solution)/shard_map/all_gather | solution.py:40
  11.5 199.1 %all-gather.9.cloned.1.call-start = ((), (), s32[]{:S(2)}) async-start(), calls=%async_computation.1 | async-start | bytes 2228224 | tf_op jit(solution)/shard_map/all_gather | solution.py:40
  12.1 247.9 %all-gather.7.cloned.1.call-start = ((), (), s32[]{:S(2)}) async-start(), calls=%async_computation | async-start | bytes 2228224 | tf_op jit(solution)/shard_map/all_gather | solution.py:40
  12.7 297.4 %all-gather.17.cloned.1.call-start = ((), (), s32[]{:S(2)}) async-start(), calls=%async_computation.5 | async-start | bytes 2228224 | tf_op jit(solution)/shard_map/all_gather | solution.py:40
  310.0 12.0 %copy-start.4 = (bf16[2048,512]{1,0:T(8,128)(2,1)S(1)}, bf16[2048,512]{1,0:T(8,128)(2,1)}, u32[]{:S(2)}) copy-start(bf16[2048,512]{1,0:T(8,128)(2,1)} %all-gather.7.cloned.1.call-done) | copy-start | bytes 6291460
  322.1 2.9 copy-start.3
  323.4 3.7 copy-start.2
  323.4 14.8 %collective-permute-start = (bf16[512,512]{0,1:T(8,128)(2,1)S(1)}, bf16[512,512]{0,1:T(8,128)(2,1)S(1)}, u32[]{:S(2)}, u32[]{:S(2)}) collective-permute-start(bf16[512,512]{0,1:T(8,128)(2,1)S(1)} %get-tuple-element.18), channel_id=1, source_target_pairs={{0,16},{16,0},{32,48},{48,32},{64,80},{80,64},{96,112},{112,96},{1... | collective-permute-start | bytes 1572872 | tf_op jit(solution)/shard_map/ppermute | solution.py:12
  326.2 3.7 copy-start.1
  326.3 23.2 %collective-permute-start.2 = (bf16[512,512]{0,1:T(8,128)(2,1)S(1)}, bf16[512,512]{0,1:T(8,128)(2,1)S(1)}, u32[]{:S(2)}, u32[]{:S(2)}) collective-permute-start(bf16[512,512]{0,1:T(8,128)(2,1)S(1)} %get-tuple-element.20), channel_id=1, source_target_pairs={{0,16},{16,0},{32,48},{48,32},{64,80},{80,64},{96,112},{112,96},{1... | collective-permute-start | bytes 1572872 | tf_op jit(solution)/shard_map/ppermute | solution.py:12
  328.4 3.5 copy-start
  328.4 32.3 %collective-permute-start.4 = (bf16[512,512]{0,1:T(8,128)(2,1)S(1)}, bf16[512,512]{0,1:T(8,128)(2,1)S(1)}, u32[]{:S(2)}, u32[]{:S(2)}) collective-permute-start(bf16[512,512]{0,1:T(8,128)(2,1)S(1)} %get-tuple-element.22), channel_id=1, source_target_pairs={{0,16},{16,0},{32,48},{48,32},{64,80},{80,64},{96,112},{112,96},{1... | collective-permute-start | bytes 1572872 | tf_op jit(solution)/shard_map/ppermute | solution.py:12
  331.3 3.5 copy-start.5
  331.3 40.6 %collective-permute-start.6 = (bf16[512,512]{0,1:T(8,128)(2,1)S(1)}, bf16[512,512]{0,1:T(8,128)(2,1)S(1)}, u32[]{:S(2)}, u32[]{:S(2)}) collective-permute-start(bf16[512,512]{0,1:T(8,128)(2,1)S(1)} %get-tuple-element.24), channel_id=1, source_target_pairs={{0,16},{16,0},{32,48},{48,32},{64,80},{80,64},{96,112},{112,96},{1... | collective-permute-start | bytes 1572872 | tf_op jit(solution)/shard_map/ppermute | solution.py:12
  333.2 49.9 %collective-permute-start.8 = (bf16[512,512]{0,1:T(8,128)(2,1)S(1)}, bf16[512,512]{0,1:T(8,128)(2,1)S(1)}, u32[]{:S(2)}, u32[]{:S(2)}) collective-permute-start(bf16[512,512]{0,1:T(8,128)(2,1)S(1)} %get-tuple-element.26), channel_id=1, source_target_pairs={{0,16},{16,0},{32,48},{48,32},{64,80},{80,64},{96,112},{112,96},{1... | collective-permute-start | bytes 1572872 | tf_op jit(solution)/shard_map/ppermute | solution.py:12
  338.2 55.5 %collective-permute-start.10 = (bf16[512,512]{0,1:T(8,128)(2,1)S(1)}, bf16[512,512]{0,1:T(8,128)(2,1)S(1)}, u32[]{:S(2)}, u32[]{:S(2)}) collective-permute-start(bf16[512,512]{0,1:T(8,128)(2,1)S(1)} %get-tuple-element.28), channel_id=1, source_target_pairs={{0,16},{16,0},{32,48},{48,32},{64,80},{80,64},{96,112},{112,96},{1... | collective-permute-start | bytes 1572872 | tf_op jit(solution)/shard_map/ppermute | solution.py:12
  349.5 47.1 %collective-permute-start.1 = (bf16[512,512]{0,1:T(8,128)(2,1)S(1)}, bf16[512,512]{0,1:T(8,128)(2,1)S(1)}, u32[]{:S(2)}, u32[]{:S(2)}) collective-permute-start(bf16[512,512]{0,1:T(8,128)(2,1)S(1)} %fusion.10), channel_id=1, source_target_pairs={{0,48},{16,32},{32,16},{48,0},{64,112},{80,96},{96,80},{112,64},{1... | collective-permute-start | bytes 1572872 | tf_op jit(solution)/shard_map/ppermute | solution.py:12
  360.7 37.0 %collective-permute-start.3 = (bf16[512,512]{0,1:T(8,128)(2,1)S(1)}, bf16[512,512]{0,1:T(8,128)(2,1)S(1)}, u32[]{:S(2)}, u32[]{:S(2)}) collective-permute-start(bf16[512,512]{0,1:T(8,128)(2,1)S(1)} %fusion.11), channel_id=1, source_target_pairs={{0,48},{16,32},{32,16},{48,0},{64,112},{80,96},{96,80},{112,64},{1... | collective-permute-start | bytes 1572872 | tf_op jit(solution)/shard_map/ppermute | solution.py:12
  371.9 26.0 %collective-permute-start.5 = (bf16[512,512]{0,1:T(8,128)(2,1)S(1)}, bf16[512,512]{0,1:T(8,128)(2,1)S(1)}, u32[]{:S(2)}, u32[]{:S(2)}) collective-permute-start(bf16[512,512]{0,1:T(8,128)(2,1)S(1)} %fusion.12), channel_id=1, source_target_pairs={{0,48},{16,32},{32,16},{48,0},{64,112},{80,96},{96,80},{112,64},{1... | collective-permute-start | bytes 1572872 | tf_op jit(solution)/shard_map/ppermute | solution.py:12
  383.2 15.0 %collective-permute-start.7 = (bf16[512,512]{0,1:T(8,128)(2,1)S(1)}, bf16[512,512]{0,1:T(8,128)(2,1)S(1)}, u32[]{:S(2)}, u32[]{:S(2)}) collective-permute-start(bf16[512,512]{0,1:T(8,128)(2,1)S(1)} %fusion.13), channel_id=1, source_target_pairs={{0,48},{16,32},{32,16},{48,0},{64,112},{80,96},{96,80},{112,64},{1... | collective-permute-start | bytes 1572872 | tf_op jit(solution)/shard_map/ppermute | solution.py:12
  393.7 16.1 %collective-permute-start.9 = (bf16[512,512]{0,1:T(8,128)(2,1)S(1)}, bf16[512,512]{0,1:T(8,128)(2,1)S(1)}, u32[]{:S(2)}, u32[]{:S(2)}) collective-permute-start(bf16[512,512]{0,1:T(8,128)(2,1)S(1)} %fusion.14), channel_id=1, source_target_pairs={{0,48},{16,32},{32,16},{48,0},{64,112},{80,96},{96,80},{112,64},{1... | collective-permute-start | bytes 1572872 | tf_op jit(solution)/shard_map/ppermute | solution.py:12
  396.6 22.8 %collective-permute-start.11 = (bf16[512,512]{0,1:T(8,128)(2,1)S(1)}, bf16[512,512]{0,1:T(8,128)(2,1)S(1)}, u32[]{:S(2)}, u32[]{:S(2)}) collective-permute-start(bf16[512,512]{0,1:T(8,128)(2,1)S(1)} %fusion.15), channel_id=1, source_target_pairs={{0,48},{16,32},{32,16},{48,0},{64,112},{80,96},{96,80},{112,64},{1... | collective-permute-start | bytes 1572872 | tf_op jit(solution)/shard_map/ppermute | solution.py:12
  (2 other events, 4.7 us)
Sparse Core Ops, SparseCore 0:
  11.0 50.9 all-gather.14
  64.4 47.0 all-gather.12
  114.0 47.0 all-gather.10
  163.5 47.0 all-gather.8
  212.9 47.0 all-gather.6
  262.9 47.0 all-gather.16
where the time goes:
time: 442 us; the launch traced here: 441 us
  waiting for transfers between devices  327 us (74%)
  matrix products  44.1 us (10%)
  starting transfers between devices  22.1 us (5%)
  between operations  17.6 us (4%)
  local copies, waits for them, and re-layouts  15.8 us (4%)
  other arithmetic  14.4 us (3%)
    all_gather x6, waiting for transfers between devices, per_device(): rows = lax.all_gather(masked[:, cols], 'shard', axis=0, tiled=True)  259 us
    ppermute x12, waiting for transfers between devices, from_partner(): lax.ppermute(shard, axis, [(i, i ^ flip) for i in range(lax.axis_size(axi...  65.3 us
    dot_general x6, matrix products, per_device(): lax.dot_general(rows, weight_work[:, cols], (((1,), (1,)), ((), ())), pre...  36.3 us
    ppermute x12, starting transfers between devices, from_partner(): lax.ppermute(shard, axis, [(i, i ^ flip) for i in range(lax.axis_size(axi...  21.9 us
    unnamed x18, local copies, waits for them, and re-layouts  14.9 us
  transfers between devices with their start and end apart: 18, of which 14 were waited for; matrix products, arithmetic and copies ran while one was open for 10% of the time, Pallas kernels for 0%

commit v1 on v0

--- a/solution.py
+++ b/solution.py
@@ -37,7 +37,10 @@
     sums = []
     for piece in range(pieces):
         cols = slice(piece * step, (piece + 1) * step)
-        rows = lax.all_gather(masked[:, cols], "shard", axis=0, tiled=True)
+        rows = jnp.concatenate(
+            lax.all_to_all(jnp.stack([masked[:, cols]] * lax.axis_size("shard")), "shard", 0, 0),
+            axis=0,
+        )
         grad = lax.dot_general(
             hidden, rows, (((0,), (0,)), ((), ())), preferred_element_type=jnp.float32
         )

time: 442 us -> 328 us (0.74)
  waiting for transfers between devices: 327 us -> 75.6 us
  blocking collectives: 0 us -> 102 us
  other arithmetic: 14.4 us -> 36.3 us
  between operations: 17.6 us -> 4.16 us
  starting transfers between devices: 22.1 us -> 35 us
  matrix products: 44.1 us -> 55 us
    all_gather x6 -> x0, waiting for transfers between devices: 259 us -> none  [per_device(): rows = lax.all_gather(masked[:, cols], 'shard', axis=0, tiled=True)]
    all_to_all x0 -> x3, blocking collectives: none -> 102 us  [per_device(): lax.all_to_all(jnp.stack([masked[:, cols]] * lax.axis_size('shard')), 'sh...]
    all_to_all x0 -> x3, waiting for transfers between devices: none -> 27.5 us  [per_device(): lax.all_to_all(jnp.stack([masked[:, cols]] * lax.axis_size('shard')), 'sh...]
    ppermute x12, waiting for transfers between devices: 65.3 us -> 48.1 us  [from_partner(): lax.ppermute(shard, axis, [(i, i ^ flip) for i in range(lax.axis_size(axi...]
    all_to_all x0 -> x3, starting transfers between devices: none -> 16.6 us  [per_device(): lax.all_to_all(jnp.stack([masked[:, cols]] * lax.axis_size('shard')), 'sh...]
    dot_general x6, matrix products: 7.84 us -> 20.8 us  [per_device(): lax.dot_general(hidden, rows, (((0,), (0,)), ((), ())), preferred_element...]
    unnamed x11, other arithmetic: 2.33 us -> 13 us
    convert_element_type x6, other arithmetic: 0.98 us -> 6.31 us  [per_device(): received = from_partner(grad.astype(jnp.bfloat16), 'expert', flip)]
  transfers between devices with their start and end apart: 18 -> 15, of which waited for: 14 -> 8; matrix products, arithmetic and copies ran while one was open for 10% -> 26% of each run, Pallas kernels for 0% -> 0%
where the time goes in v1:
time: 328 us; the launch traced here: 326 us
  blocking collectives  102 us (31%)
  waiting for transfers between devices  75.6 us (23%)
  matrix products  55 us (17%)
  other arithmetic  36.3 us (11%)
  starting transfers between devices  35 us (11%)
  local copies, waits for them, and re-layouts  18.4 us (6%)
  between operations  4.16 us (1%)
    all_to_all x3, blocking collectives, per_device(): lax.all_to_all(jnp.stack([masked[:, cols]] * lax.axis_size('shard')), 'sh...  102 us
    ppermute x12, waiting for transfers between devices, from_partner(): lax.ppermute(shard, axis, [(i, i ^ flip) for i in range(lax.axis_size(axi...  48.1 us
    dot_general x6, matrix products, per_device(): lax.dot_general(rows, weight_work[:, cols], (((1,), (1,)), ((), ())), pre...  34.2 us
    all_to_all x3, waiting for transfers between devices, per_device(): lax.all_to_all(jnp.stack([masked[:, cols]] * lax.axis_size('shard')), 'sh...  27.5 us
    dot_general x6, matrix products, per_device(): lax.dot_general(hidden, rows, (((0,), (0,)), ((), ())), preferred_element...  20.8 us
    ppermute x12, starting transfers between devices, from_partner(): lax.ppermute(shard, axis, [(i, i ^ flip) for i in range(lax.axis_size(axi...  18.4 us
    all_to_all x3, starting transfers between devices, per_device(): lax.all_to_all(jnp.stack([masked[:, cols]] * lax.axis_size('shard')), 'sh...  16.6 us
    unnamed x30, local copies, waits for them, and re-layouts  13.2 us
  transfers between devices with their start and end apart: 15, of which 8 were waited for; matrix products, arithmetic and copies ran while one was open for 26% of the time, Pallas kernels for 0%

profile of v1, /device:TPU:0, one launch (start us, length us, event | category | flops | bytes accessed | tf_op | source)
XLA Modules:
  0.0 326.5 jit_solution(318354785081448647)
XLA Ops:
  2.8 37.0 %all_to_all.30 = bf16[16,128,512]{2,1,0:T(8,128)(2,1)S(1)} all-to-all(bf16[16,128,512]{2,1,0:T(8,128)(2,1)S(1)} %stack.12), channel_id=1, replica_groups=mesh['expert'=8,'shard'=16] {'shard'}, dimensions={0} | all-to-all | bytes 4194304 | tf_op jit(solution)/shard_map/all_to_all | solution.py:41
  40.0 32.5 %all_to_all.31 = bf16[16,128,512]{2,1,0:T(8,128)(2,1)} all-to-all(bf16[16,128,512]{2,1,0:T(8,128)(2,1)S(1)} %stack.13), channel_id=1, replica_groups=mesh['expert'=8,'shard'=16] {'shard'}, dimensions={0} | all-to-all | bytes 4194304 | tf_op jit(solution)/shard_map/all_to_all | solution.py:41
  72.8 32.5 %all_to_all.32 = bf16[16,128,512]{2,1,0:T(8,128)(2,1)} all-to-all(bf16[16,128,512]{2,1,0:T(8,128)(2,1)S(1)} %stack.14), channel_id=1, replica_groups=mesh['expert'=8,'shard'=16] {'shard'}, dimensions={0} | all-to-all | bytes 4194304 | tf_op jit(solution)/shard_map/all_to_all | solution.py:41
  106.8 4.4 %all-to-all-start.3 = ((bf16[16,128,512]{2,1,0:T(8,128)(2,1)}), bf16[16,128,512]{2,1,0:T(8,128)(2,1)}, u32[]{:S(2)}, u32[]{:S(2)}) async-start(bf16[16,128,512]{2,1,0:T(8,128)(2,1)} %stack.15), calls=%async_computation.3 | async-start | bytes 4194304 | tf_op jit(solution)/shard_map/all_to_all | solution.py:41
  111.3 4.9 %convert_bitcast_fusion.2 = bf16[512,3072]{1,0:T(8,128)(2,1)} fusion(f32[1,512,3072]{2,1,0:T(8,128)} %param.11), kind=kLoop, calls=%fused_computation.25 | loop fusion | flops 1572864 | bytes 9437184 | tf_op jit(solution)/shard_map/convert_element_type | solution.py:16
  116.2 24.3 %all-to-all-done.3 = bf16[16,128,512]{2,1,0:T(8,128)(2,1)} async-done(((bf16[16,128,512]{2,1,0:T(8,128)(2,1)}), bf16[16,128,512]{2,1,0:T(8,128)(2,1)}, u32[]{:S(2)}, u32[]{:S(2)}) %all-to-all-start.3) | async-done | bytes 2097184 | tf_op jit(solution)/shard_map/all_to_all | solution.py:41
  142.0 4.9 %all-to-all-start.4 = ((bf16[16,128,512]{2,1,0:T(8,128)(2,1)}), bf16[16,128,512]{2,1,0:T(8,128)(2,1)}, u32[]{:S(2)}, u32[]{:S(2)}) async-start(bf16[16,128,512]{2,1,0:T(8,128)(2,1)} %stack.16), calls=%async_computation.4 | async-start | bytes 4194304 | tf_op jit(solution)/shard_map/all_to_all | solution.py:41
  147.0 4.9 %fusion.6 = bf16[1,2048,512]{2,1,0:T(8,128)(2,1)} fusion(bf16[1,2048,512]{2,1,0:T(8,128)(2,1)} %param.8, bf16[1,2048,512]{2,1,0:T(8,128)(2,1)} %param.7), kind=kLoop, calls=%fused_computation.13 | loop fusion | flops 8388608 | bytes 6291456 | tf_op jit(solution)/shard_map/convert_element_type | solution.py:25
  151.8 6.6 %copy.9 = f32[1,512,3072]{1,2,0:T(8,128)} copy(f32[1,512,3072]{2,1,0:T(8,128)} %param.11) | data formatting | bytes 12582912 | tf_op args[5]
  161.7 3.8 %fusion.58 = (bf16[512,512]{0,1:T(8,128)(2,1)}, f32[512,512]{0,1:T(8,128)S(1)}) fusion(bf16[2048,512]{1,0:T(8,128)(2,1)S(1)} %bitcast.109, bf16[1,2048,512]{2,1,0:T(8,128)(2,1)} %fusion.6), kind=kOutput, calls=%fused_computation.91 | convolution fusion | flops 1074003968 | bytes 5767168 | tf_op jit(solution)/shard_map/dot_general | solution.py:44
  174.1 4.1 %fusion.61 = (bf16[512,512]{0,1:T(8,128)(2,1)}, f32[512,512]{0,1:T(8,128)}) fusion(bf16[2048,512]{1,0:T(8,128)(2,1)} %bitcast.6, bf16[1,2048,512]{2,1,0:T(8,128)(2,1)S(1)} %copy-done.9), kind=kOutput, calls=%fused_computation.94 | convolution fusion | flops 1074003968 | bytes 5767168 | tf_op jit(solution)/shard_map/dot_general | solution.py:44
  180.2 7.2 %all-to-all-start.5 = ((bf16[16,128,512]{2,1,0:T(8,128)(2,1)}), bf16[16,128,512]{2,1,0:T(8,128)(2,1)}, u32[]{:S(2)}, u32[]{:S(2)}) async-start(bf16[16,128,512]{2,1,0:T(8,128)(2,1)} %stack.17), calls=%async_computation.5 | async-start | bytes 4194304 | tf_op jit(solution)/shard_map/all_to_all | solution.py:41
  187.4 4.9 %fusion.62 = (bf16[512,512]{0,1:T(8,128)(2,1)}, f32[512,512]{0,1:T(8,128)}) fusion(bf16[2048,512]{1,0:T(8,128)(2,1)} %bitcast.7, bf16[1,2048,512]{2,1,0:T(8,128)(2,1)} %fusion.6), kind=kOutput, calls=%fused_computation.95 | convolution fusion | flops 1074003968 | bytes 5767168 | tf_op jit(solution)/shard_map/dot_general | solution.py:44
  193.8 4.8 %fusion.38 = f32[2048,512]{1,0:T(8,128)} fusion(bf16[2048,512]{1,0:T(8,128)(2,1)} %bitcast.7, bf16[512,3072]{1,0:T(8,128)(2,1)S(1)} %copy-done.4), kind=kOutput, calls=%fused_computation.66 | convolution fusion | flops 1073741824 | bytes 6815744 | tf_op jit(solution)/shard_map/dot_general | solution.py:51
  198.6 5.0 %fusion.40 = f32[2048,512]{1,0:T(8,128)} fusion(bf16[2048,512]{1,0:T(8,128)(2,1)} %bitcast.6, bf16[512,3072]{1,0:T(8,128)(2,1)S(1)} %copy-done.4), kind=kOutput, calls=%fused_computation.68 | convolution fusion | flops 1073741824 | bytes 6815744 | tf_op jit(solution)/shard_map/dot_general | solution.py:51
  203.7 3.3 %fusion.42 = f32[2048,512]{1,0:T(8,128)} fusion(bf16[2048,512]{1,0:T(8,128)(2,1)S(1)} %bitcast.114, bf16[512,3072]{1,0:T(8,128)(2,1)S(1)} %copy-done.4), kind=kOutput, calls=%fused_computation.70 | convolution fusion | flops 1073741824 | bytes 6815744 | tf_op jit(solution)/shard_map/dot_general | solution.py:51
  216.7 14.5 %fusion.29 = (bf16[1,2048,512]{2,1,0:T(8,128)(2,1)}, bf16[1,2048,512]{2,1,0:T(8,128)(2,1)}) fusion(bf16[1,2048,512]{2,1,0:T(8,128)(2,1)} %param.7, bf16[1,2048,512]{2,1,0:T(8,128)(2,1)} %param.8, bf16[2048,512]{1,0:T(8,128)(2,1)} %bitcast.8, bf16[512,3072]{1,0:T(8,128)(2,1)} %convert_bitcast_fusion.2, f32[2048,512]{1,0:T(8,128)} %fusion.38, ...), kind=kOutput, calls=%fused_computation.38 | convolution fusion | flops 1094713344 | bytes 31981568 | tf_op jit(solution)/shard_map/dot_general | solution.py:51
  256.7 7.9 %collective-permute-done.3 = bf16[512,512]{0,1:T(8,128)(2,1)S(1)} collective-permute-done((bf16[512,512]{0,1:T(8,128)(2,1)S(1)}, bf16[512,512]{0,1:T(8,128)(2,1)S(1)}, u32[]{:S(2)}, u32[]{:S(2)}) %collective-permute-start.3) | collective-permute-done | bytes 524320 | tf_op jit(solution)/shard_map/ppermute | solution.py:12
  265.8 10.0 %collective-permute-done.5 = bf16[512,512]{0,1:T(8,128)(2,1)S(1)} collective-permute-done((bf16[512,512]{0,1:T(8,128)(2,1)S(1)}, bf16[512,512]{0,1:T(8,128)(2,1)S(1)}, u32[]{:S(2)}, u32[]{:S(2)}) %collective-permute-start.5) | collective-permute-done | bytes 524320 | tf_op jit(solution)/shard_map/ppermute | solution.py:12
  277.1 10.0 %collective-permute-done.7 = bf16[512,512]{0,1:T(8,128)(2,1)S(1)} collective-permute-done((bf16[512,512]{0,1:T(8,128)(2,1)S(1)}, bf16[512,512]{0,1:T(8,128)(2,1)S(1)}, u32[]{:S(2)}, u32[]{:S(2)}) %collective-permute-start.7) | collective-permute-done | bytes 524320 | tf_op jit(solution)/shard_map/ppermute | solution.py:12
  288.3 10.0 %collective-permute-done.9 = bf16[512,512]{0,1:T(8,128)(2,1)S(1)} collective-permute-done((bf16[512,512]{0,1:T(8,128)(2,1)S(1)}, bf16[512,512]{0,1:T(8,128)(2,1)S(1)}, u32[]{:S(2)}, u32[]{:S(2)}) %collective-permute-start.9) | collective-permute-done | bytes 524320 | tf_op jit(solution)/shard_map/ppermute | solution.py:12
  299.5 8.4 %collective-permute-done.11 = bf16[512,512]{0,1:T(8,128)(2,1)S(1)} collective-permute-done((bf16[512,512]{0,1:T(8,128)(2,1)S(1)}, bf16[512,512]{0,1:T(8,128)(2,1)S(1)}, u32[]{:S(2)}, u32[]{:S(2)}) %collective-permute-start.11) | collective-permute-done | bytes 524320 | tf_op jit(solution)/shard_map/ppermute | solution.py:12
  315.7 4.2 %divide_subtract_fusion = f32[1,512,3072]{1,2,0:T(8,128)} fusion(f32[1,512,3072]{1,2,0:T(8,128)S(1)} %bitcast.108, f32[1,512,3072]{1,2,0:T(8,128)S(1)} %bitcast_dynamic-update-slice_fusion, f32[512]{0:T(512)S(1)} %add_sqrt_fusion), kind=kLoop, calls=%fused_computation.6 | loop fusion | flops 4718592 | bytes 18876416 | tf_op jit(solution)/shard_map/sub | solution.py:58
  319.9 6.6 %copy.10 = f32[1,512,3072]{2,1,0:T(8,128)} copy(f32[1,512,3072]{1,2,0:T(8,128)} %divide_subtract_fusion) | data formatting | bytes 12582912
  (85 shorter events, 65.5 us)
Async XLA Ops:
  106.8 33.7 %all-to-all-start.3 = ((bf16[16,128,512]{2,1,0:T(8,128)(2,1)}), bf16[16,128,512]{2,1,0:T(8,128)(2,1)}, u32[]{:S(2)}, u32[]{:S(2)}) async-start(bf16[16,128,512]{2,1,0:T(8,128)(2,1)} %stack.15), calls=%async_computation.3 | async-start | bytes 4194304 | tf_op jit(solution)/shard_map/all_to_all | solution.py:41
  142.0 36.6 %all-to-all-start.4 = ((bf16[16,128,512]{2,1,0:T(8,128)(2,1)}), bf16[16,128,512]{2,1,0:T(8,128)(2,1)}, u32[]{:S(2)}, u32[]{:S(2)}) async-start(bf16[16,128,512]{2,1,0:T(8,128)(2,1)} %stack.16), calls=%async_computation.4 | async-start | bytes 4194304 | tf_op jit(solution)/shard_map/all_to_all | solution.py:41
  151.8 6.6 %copy-start.11 = (s32[8]{0:T(128)S(1)}, s32[8]{0:T(128)}, u32[]{:S(2)}) copy-start(s32[8]{0:T(128)} %param.10) | copy-start | bytes 100
  161.7 5.4 %copy-start = (bf16[16,128,512]{2,1,0:T(8,128)(2,1)S(1)}, bf16[16,128,512]{2,1,0:T(8,128)(2,1)}, u32[]{:S(2)}) copy-start(bf16[16,128,512]{2,1,0:T(8,128)(2,1)} %all_to_all.31) | copy-start | bytes 6291460
  165.6 68.7 %collective-permute-start = (bf16[512,512]{0,1:T(8,128)(2,1)}, bf16[512,512]{0,1:T(8,128)(2,1)}, u32[]{:S(2)}, u32[]{:S(2)}) collective-permute-start(bf16[512,512]{0,1:T(8,128)(2,1)} %get-tuple-element.17), channel_id=1, source_target_pairs={{0,16},{16,0},{32,48},{48,32},{64,80},{80,64},{96,112},{112,96},{1... | collective-permute-start | bytes 1572872 | tf_op jit(solution)/shard_map/ppermute | solution.py:12
  169.6 67.6 %collective-permute-start.2 = (bf16[512,512]{0,1:T(8,128)(2,1)}, bf16[512,512]{0,1:T(8,128)(2,1)}, u32[]{:S(2)}, u32[]{:S(2)}) collective-permute-start(bf16[512,512]{0,1:T(8,128)(2,1)} %get-tuple-element.19), channel_id=1, source_target_pairs={{0,16},{16,0},{32,48},{48,32},{64,80},{80,64},{96,112},{112,96},{1... | collective-permute-start | bytes 1572872 | tf_op jit(solution)/shard_map/ppermute | solution.py:12
  172.6 68.0 %collective-permute-start.4 = (bf16[512,512]{0,1:T(8,128)(2,1)}, bf16[512,512]{0,1:T(8,128)(2,1)}, u32[]{:S(2)}, u32[]{:S(2)}) collective-permute-start(bf16[512,512]{0,1:T(8,128)(2,1)} %get-tuple-element.21), channel_id=1, source_target_pairs={{0,16},{16,0},{32,48},{48,32},{64,80},{80,64},{96,112},{112,96},{1... | collective-permute-start | bytes 1572872 | tf_op jit(solution)/shard_map/ppermute | solution.py:12
  178.1 64.9 %collective-permute-start.6 = (bf16[512,512]{0,1:T(8,128)(2,1)}, bf16[512,512]{0,1:T(8,128)(2,1)}, u32[]{:S(2)}, u32[]{:S(2)}) collective-permute-start(bf16[512,512]{0,1:T(8,128)(2,1)} %get-tuple-element.23), channel_id=1, source_target_pairs={{0,16},{16,0},{32,48},{48,32},{64,80},{80,64},{96,112},{112,96},{1... | collective-permute-start | bytes 1572872 | tf_op jit(solution)/shard_map/ppermute | solution.py:12
  180.2 36.5 %all-to-all-start.5 = ((bf16[16,128,512]{2,1,0:T(8,128)(2,1)}), bf16[16,128,512]{2,1,0:T(8,128)(2,1)}, u32[]{:S(2)}, u32[]{:S(2)}) async-start(bf16[16,128,512]{2,1,0:T(8,128)(2,1)} %stack.17), calls=%async_computation.5 | async-start | bytes 4194304 | tf_op jit(solution)/shard_map/all_to_all | solution.py:41
  187.4 6.4 %copy-start.4 = (bf16[512,3072]{1,0:T(8,128)(2,1)S(1)}, bf16[512,3072]{1,0:T(8,128)(2,1)}, u32[]{:S(2)}) copy-start(bf16[512,3072]{1,0:T(8,128)(2,1)} %convert_bitcast_fusion.2) | copy-start | bytes 9437188
  192.3 54.3 %collective-permute-start.8 = (bf16[512,512]{0,1:T(8,128)(2,1)}, bf16[512,512]{0,1:T(8,128)(2,1)}, u32[]{:S(2)}, u32[]{:S(2)}) collective-permute-start(bf16[512,512]{0,1:T(8,128)(2,1)} %get-tuple-element.25), channel_id=1, source_target_pairs={{0,16},{16,0},{32,48},{48,32},{64,80},{80,64},{96,112},{112,96},{1... | collective-permute-start | bytes 1572872 | tf_op jit(solution)/shard_map/ppermute | solution.py:12
  216.7 14.5 %copy-start.10 = (bf16[1,2048,512]{2,1,0:T(8,128)(2,1)S(1)}, bf16[1,2048,512]{2,1,0:T(8,128)(2,1)}, u32[]{:S(2)}) copy-start(bf16[1,2048,512]{2,1,0:T(8,128)(2,1)} %fusion.6) | copy-start | bytes 6291460
  231.2 8.1 %copy-start.5 = (f32[512,512]{0,1:T(8,128)S(1)}, f32[512,512]{0,1:T(8,128)}, u32[]{:S(2)}) copy-start(f32[512,512]{0,1:T(8,128)} %get-tuple-element.20) | copy-start | bytes 3145732
  231.2 10.6 %copy-start.6 = (f32[512,512]{0,1:T(8,128)S(1)}, f32[512,512]{0,1:T(8,128)}, u32[]{:S(2)}) copy-start(f32[512,512]{0,1:T(8,128)} %get-tuple-element.22) | copy-start | bytes 3145732
  234.3 11.1 %copy-start.7 = (f32[512,512]{0,1:T(8,128)S(1)}, f32[512,512]{0,1:T(8,128)}, u32[]{:S(2)}) copy-start(f32[512,512]{0,1:T(8,128)} %get-tuple-element.24) | copy-start | bytes 3145732
  234.3 14.8 %collective-permute-start.10 = (bf16[512,512]{0,1:T(8,128)(2,1)S(1)}, bf16[512,512]{0,1:T(8,128)(2,1)S(1)}, u32[]{:S(2)}, u32[]{:S(2)}) collective-permute-start(bf16[512,512]{0,1:T(8,128)(2,1)S(1)} %get-tuple-element.27), channel_id=1, source_target_pairs={{0,16},{16,0},{32,48},{48,32},{64,80},{80,64},{96,112},{112,96},{1... | collective-permute-start | bytes 1572872 | tf_op jit(solution)/shard_map/ppermute | solution.py:12
  235.9 12.0 %copy-start.8 = (f32[512,512]{0,1:T(8,128)S(1)}, f32[512,512]{0,1:T(8,128)}, u32[]{:S(2)}) copy-start(f32[512,512]{0,1:T(8,128)} %get-tuple-element.26) | copy-start | bytes 3145732
  237.2 16.1 %collective-permute-start.1 = (bf16[512,512]{0,1:T(8,128)(2,1)S(1)}, bf16[512,512]{0,1:T(8,128)(2,1)S(1)}, u32[]{:S(2)}, u32[]{:S(2)}) collective-permute-start(bf16[512,512]{0,1:T(8,128)(2,1)S(1)} %fusion.31), channel_id=1, source_target_pairs={{0,48},{16,32},{32,16},{48,0},{64,112},{80,96},{96,80},{112,64},{1... | collective-permute-start | bytes 1572872 | tf_op jit(solution)/shard_map/ppermute | solution.py:12
  240.6 24.0 %collective-permute-start.3 = (bf16[512,512]{0,1:T(8,128)(2,1)S(1)}, bf16[512,512]{0,1:T(8,128)(2,1)S(1)}, u32[]{:S(2)}, u32[]{:S(2)}) collective-permute-start(bf16[512,512]{0,1:T(8,128)(2,1)S(1)} %fusion.32), channel_id=1, source_target_pairs={{0,48},{16,32},{32,16},{48,0},{64,112},{80,96},{96,80},{112,64},{1... | collective-permute-start | bytes 1572872 | tf_op jit(solution)/shard_map/ppermute | solution.py:12
  243.0 32.8 %collective-permute-start.5 = (bf16[512,512]{0,1:T(8,128)(2,1)S(1)}, bf16[512,512]{0,1:T(8,128)(2,1)S(1)}, u32[]{:S(2)}, u32[]{:S(2)}) collective-permute-start(bf16[512,512]{0,1:T(8,128)(2,1)S(1)} %fusion.33), channel_id=1, source_target_pairs={{0,48},{16,32},{32,16},{48,0},{64,112},{80,96},{96,80},{112,64},{1... | collective-permute-start | bytes 1572872 | tf_op jit(solution)/shard_map/ppermute | solution.py:12
  246.6 40.4 %collective-permute-start.7 = (bf16[512,512]{0,1:T(8,128)(2,1)S(1)}, bf16[512,512]{0,1:T(8,128)(2,1)S(1)}, u32[]{:S(2)}, u32[]{:S(2)}) collective-permute-start(bf16[512,512]{0,1:T(8,128)(2,1)S(1)} %fusion.34), channel_id=1, source_target_pairs={{0,48},{16,32},{32,16},{48,0},{64,112},{80,96},{96,80},{112,64},{1... | collective-permute-start | bytes 1572872 | tf_op jit(solution)/shard_map/ppermute | solution.py:12
  249.1 49.2 %collective-permute-start.9 = (bf16[512,512]{0,1:T(8,128)(2,1)S(1)}, bf16[512,512]{0,1:T(8,128)(2,1)S(1)}, u32[]{:S(2)}, u32[]{:S(2)}) collective-permute-start(bf16[512,512]{0,1:T(8,128)(2,1)S(1)} %fusion.35), channel_id=1, source_target_pairs={{0,48},{16,32},{32,16},{48,0},{64,112},{80,96},{96,80},{112,64},{1... | collective-permute-start | bytes 1572872 | tf_op jit(solution)/shard_map/ppermute | solution.py:12
  253.3 54.7 %collective-permute-start.11 = (bf16[512,512]{0,1:T(8,128)(2,1)S(1)}, bf16[512,512]{0,1:T(8,128)(2,1)S(1)}, u32[]{:S(2)}, u32[]{:S(2)}) collective-permute-start(bf16[512,512]{0,1:T(8,128)(2,1)S(1)} %fusion.36), channel_id=1, source_target_pairs={{0,48},{16,32},{32,16},{48,0},{64,112},{80,96},{96,80},{112,64},{1... | collective-permute-start | bytes 1572872 | tf_op jit(solution)/shard_map/ppermute | solution.py:12
  310.0 5.7 %slice-start = ((s8[6291456]{0:T(1024)(128)(4,1)}), s8[4194304]{0:T(1024)(128)(4,1)S(1)}, s32[]{:S(2)}) async-start(s8[6291456]{0:T(1024)(128)(4,1)} %bitcast.107), calls=%async_computation.6 | async-start | bytes 8388608
  (5 other events, 21.2 us)
